TPU v7x, 128 devices: a whole 4x4x4 slice. The times are simulated.
128 devices in a mesh: dp: 4 (over y), fsdp: 4 (over x_lo, core), ctx: 8 (over z, x_hi).
Axes of the slice: x: 4 (x_hi: 2, x_lo: 2; x = x_hi * 2 + x_lo), y: 4, z: 4, core: 2. Of those that a mesh axis runs over, the one named last changes fastest.
Arguments:
- tokens: bfloat16 [16, 4096, 1024], P(('dp', 'fsdp'), 'ctx')
- bounds: int32 [16, 4096], P(('dp', 'fsdp'), 'ctx'), may hold values 0 or 1
- decay_rates: float32 [16], replicated, may hold values from 2.4414063e-05 to 0.9
- w_query: bfloat16 [1024, 1024], P('fsdp')
- w_key: bfloat16 [1024, 1024], P('fsdp')
- w_up: bfloat16 [1024, 2048], P('fsdp'), may hold values from -0.1875 to 0.1875
- grad_out: bfloat16 [16, 4096, 2048], P(('dp', 'fsdp'), 'ctx'), may hold values from -6 to 6
Outputs:
- dechunked: bfloat16 [16, 4096, 2048], P(('dp', 'fsdp'), 'ctx')
- grad_tokens: bfloat16 [16, 4096, 1024], P(('dp', 'fsdp'), 'ctx')
- grad_query: float32 [1024, 1024], P('fsdp')
- grad_key: float32 [1024, 1024], P('fsdp')
- grad_up: float32 [1024, 2048], P('fsdp')
All inputs are finite; a program needn't handle non-finite values. No bound on the sum of `bounds` on one device may be relied on, other than what follows from the above.
Results may differ from a plain program's by a relative error of at most 0.0049.
Values may be sent and summed in bfloat16 or wider, within the bound.
No kernel may reach another device: no remote copies, remote signals or barrier semaphores. Data moves between devices by JAX's collectives and lax.ppermute only.
A program may use at most 128 MiB of HBM per device.

v0:
```python
import jax
import jax.numpy as jnp
from jax import lax
from jax.sharding import PartitionSpec as P

SPAN = 128
epsilon = 1e-06


def shifted(x, axis, by):
    devices = lax.axis_size(axis)
    pairs = [(i, i + by) for i in range(devices) if 0 <= i + by < devices]
    return lax.ppermute(x, axis, pairs)


def carried_in(part, axis, combine, identity, reverse):
    count = lax.axis_size(axis)
    place = lax.axis_index(axis)
    ahead = count - 1 - place if reverse else place
    gathered = jax.tree.map(lambda a: lax.all_gather(a, axis), part)
    state = jax.tree.map(lambda a, e: jnp.zeros_like(a) + jnp.asarray(e, a.dtype), part, identity)

    def one(turn, state):
        source = count - 1 - turn if reverse else turn
        return combine(
            state, jax.tree.map(lambda a: lax.dynamic_index_in_dim(a, source, 0, False), gathered)
        )

    return lax.fori_loop(0, ahead, one, state)


def chain_pair(earlier, latter):
    decay_first, state_first = earlier
    decay_second, state_second = latter
    return (decay_first * decay_second, decay_second[..., None] * state_first + state_second)


def per_device(tokens, bounds, decay_rates, w_query, w_key, w_up, grad_out):
    batch_local, length, model_width = tokens.shape
    hidden = w_up.shape[1]
    head_count = decay_rates.shape[0]
    channels = hidden // head_count
    blocks = length // SPAN
    columns_all = 2 * model_width + hidden
    flat_tokens = tokens.reshape(batch_local * length, model_width)
    panels = jnp.concatenate([w_query, w_key, w_up], 1)
    full_panels = lax.all_gather(panels, "fsdp", axis=0, tiled=True)
    projected = jnp.dot(flat_tokens, full_panels, preferred_element_type=jnp.float32)
    queries = projected[:, :model_width].reshape(batch_local, length, model_width)
    keys_now = projected[:, model_width : 2 * model_width].reshape(batch_local, length, model_width)
    values = projected[:, 2 * model_width :].reshape(
        batch_local, blocks, SPAN, head_count, channels
    )
    key_before = shifted(keys_now[:, -1:, :], "ctx", 1)
    keys_prev = jnp.concatenate([key_before, keys_now[:, :-1]], 1)
    inv_query = lax.rsqrt(jnp.sum(queries * queries, -1) + epsilon)
    inv_key = lax.rsqrt(jnp.sum(keys_prev * keys_prev, -1) + epsilon)
    cosine = jnp.sum(queries * keys_prev, -1) * inv_query * inv_key
    own_index = lax.axis_index("ctx")
    opening = jnp.logical_and(own_index == 0, jnp.arange(length) == 0)[None, :]
    boundary_prob = jnp.where(opening, 1.0, 0.5 * (1.0 - cosine))
    marked = jnp.where(opening, 1.0, bounds.astype(jnp.float32))
    mix_rate = (marked * boundary_prob)[..., None] * decay_rates
    rate_blocks = mix_rate.reshape(batch_local, blocks, SPAN, head_count)
    log_keep = jnp.cumsum(jnp.log(1.0 - rate_blocks), axis=2)
    keep_heads = jnp.moveaxis(log_keep, 3, 2)
    log_gap = keep_heads[..., :, None] - keep_heads[..., None, :]
    offsets = jnp.arange(SPAN)
    lower_mask = offsets[:, None] >= offsets[None, :]
    upper_mask = offsets[:, None] <= offsets[None, :]
    forward_band = (
        jnp.where(lower_mask, jnp.exp(jnp.where(lower_mask, log_gap, -1e30)), 0.0)
        * jnp.moveaxis(rate_blocks, 3, 2)[..., None, :]
    )
    local_states = jnp.einsum(
        "bnhtu,bnuhc->bnthc", forward_band, values, precision=lax.Precision.HIGHEST
    )
    block_logs = log_keep[:, :, -1]
    block_decay = jnp.exp(block_logs)
    running_logs = jnp.cumsum(block_logs, axis=1)
    decay_before = jnp.exp(running_logs - block_logs)
    decay_after = jnp.exp(running_logs[:, -1:] - running_logs)
    device_decay = jnp.exp(running_logs[:, -1])
    inner_zero = jnp.zeros((batch_local, head_count, channels), jnp.float32)

    def walk_blocks(carried, element):
        decay_now, addition = element
        return (decay_now[..., None] * carried + addition, carried)

    device_state, block_in = lax.scan(
        walk_blocks,
        inner_zero,
        (jnp.moveaxis(block_decay, 1, 0), jnp.moveaxis(local_states[:, :, -1], 1, 0)),
    )
    identity_pair = (jnp.ones_like(device_decay), inner_zero)
    _, state_in = carried_in((device_decay, device_state), "ctx", chain_pair, identity_pair, False)
    block_carry = jnp.moveaxis(block_in, 0, 1) + decay_before[..., None] * state_in[:, None]
    states = local_states + jnp.exp(log_keep)[..., None] * block_carry[:, :, None]
    dechunked = states.reshape(batch_local, length, hidden).astype(jnp.bfloat16)
    state_rows = states.reshape(batch_local, length, head_count, channels)
    states_prev = jnp.concatenate([state_in[:, None], state_rows[:, :-1]], 1)
    cotangent = grad_out.astype(jnp.float32).reshape(
        batch_local, blocks, SPAN, head_count, channels
    )
    backward_band = jnp.where(upper_mask, jnp.exp(jnp.where(upper_mask, -log_gap, -1e30)), 0.0)
    local_adjoint = jnp.einsum(
        "bnhtu,bnuhc->bnthc", backward_band, cotangent, precision=lax.Precision.HIGHEST
    )
    block_heads = (1.0 - rate_blocks[:, :, 0])[..., None] * local_adjoint[:, :, 0]
    device_head, block_out = lax.scan(
        walk_blocks,
        inner_zero,
        (jnp.moveaxis(block_decay, 1, 0), jnp.moveaxis(block_heads, 1, 0)),
        reverse=True,
    )
    _, adjoint_in = carried_in((device_decay, device_head), "ctx", chain_pair, identity_pair, True)
    block_from = jnp.moveaxis(block_out, 0, 1) + decay_after[..., None] * adjoint_in[:, None]
    adjoints = (
        local_adjoint + jnp.exp(log_keep[:, :, -1:] - log_keep)[..., None] * block_from[:, :, None]
    )
    adjoint_rows = adjoints.reshape(batch_local, length, head_count, channels)
    d_values = (
        (mix_rate[..., None] * adjoint_rows)
        .reshape(batch_local, length, hidden)
        .astype(jnp.bfloat16)
    )
    value_rows = values.reshape(batch_local, length, head_count, channels)
    d_rate = jnp.sum(adjoint_rows * (value_rows - states_prev), -1)
    d_prob = jnp.where(opening, 0.0, marked * jnp.sum(d_rate * decay_rates, -1))
    d_cos = -0.5 * d_prob
    pair_scale = inv_query * inv_key
    d_query = (
        d_cos[..., None]
        * (
            keys_prev * pair_scale[..., None]
            - (cosine * inv_query * inv_query)[..., None] * queries
        )
    ).astype(jnp.bfloat16)
    d_prev = d_cos[..., None] * (
        queries * pair_scale[..., None] - (cosine * inv_key * inv_key)[..., None] * keys_prev
    )
    key_after = shifted(d_prev[:, :1, :], "ctx", -1)
    d_key = jnp.concatenate([d_prev[:, 1:], key_after], 1).astype(jnp.bfloat16)
    d_all = jnp.concatenate([d_query, d_key, d_values], 2).reshape(
        batch_local * length, columns_all
    )
    d_flat = lax.dot_general(
        d_all, full_panels, (((1,), (1,)), ((), ())), preferred_element_type=jnp.float32
    )
    grad_tokens = d_flat.reshape(batch_local, length, model_width).astype(jnp.bfloat16)
    grads = lax.dot_general(
        flat_tokens, d_all, (((0,), (0,)), ((), ())), preferred_element_type=jnp.float32
    )
    reduced = lax.psum_scatter(grads, "fsdp", scatter_dimension=0, tiled=True)
    summed = lax.psum(reduced, ("dp", "ctx"))
    return (
        dechunked,
        grad_tokens,
        summed[:, :model_width],
        summed[:, model_width : 2 * model_width],
        summed[:, 2 * model_width :],
    )


def solution(mesh):
    return jax.shard_map(
        per_device,
        mesh=mesh,
        in_specs=(
            P(("dp", "fsdp"), "ctx", None),
            P(("dp", "fsdp"), "ctx"),
            P(),
            P("fsdp", None),
            P("fsdp", None),
            P("fsdp", None),
            P(("dp", "fsdp"), "ctx", None),
        ),
        out_specs=(
            P(("dp", "fsdp"), "ctx", None),
            P(("dp", "fsdp"), "ctx", None),
            P("fsdp", None),
            P("fsdp", None),
            P("fsdp", None),
        ),
        check_vma=False,
    )
```

profile of v0, /device:TPU:0, one launch (start us, length us, event | category | flops | bytes accessed | tf_op | source)
XLA Modules:
  0.0 855.9 jit_solution(13481682281090934830)
XLA Ops:
  7.2 3.2 pad_maximum_fusion.2
  13.1 79.9 %all-gather.4.cloned.1.call-done = bf16[1024,4096]{1,0:T(8,128)(2,1)} async-done(((bf16[256,4096]{1,0:T(8,128)(2,1)}), bf16[1024,4096]{1,0:T(8,128)(2,1)}) %all-gather.4.cloned.1.call-update) | async-done | bytes 8388624 | tf_op jit(solution)/shard_map/all_gather | solution.py:47
  93.1 6.9 convolution_bitcast_fusion.1
  100.7 4.6 collective-permute-start
  105.6 2.9 copy.153
  113.6 7.8 fusion.21
  123.4 2.9 while.58
  126.3 34.6 %all-gather = f32[8,16,128]{2,1,0:T(8,128)S(1)} all-gather(f32[1,16,128]{2,1,0:T(8,128)S(1)} %get-tuple-element.266), channel_id=2, replica_groups=mesh['dp'=4,'fsdp'=4,'ctx'=8] {'ctx'}, dimensions={0}, use_global_device_ids=true | all-gather | bytes 73728 | tf_op jit(solution)/shard_map/all_gather | solution.py:20
  162.2 22.3 %all_gather.22 = f32[8,1,16]{2,1,0:T(1,128)} all-gather(f32[1,1,16]{2,1,0:T(1,128)S(1)} %get-tuple-element.521), channel_id=1, replica_groups=mesh['dp'=4,'fsdp'=4,'ctx'=8] {'ctx'}, dimensions={0}, use_global_device_ids=true | all-gather | bytes 576 | tf_op jit(solution)/shard_map/all_gather | solution.py:20
  187.4 5.0 fusion.18
  194.6 2.9 while.59
  197.5 35.0 %all-gather.1 = f32[8,16,128]{2,1,0:T(8,128)S(1)} all-gather(f32[1,16,128]{2,1,0:T(8,128)S(1)} %get-tuple-element.269), channel_id=3, replica_groups=mesh['dp'=4,'fsdp'=4,'ctx'=8] {'ctx'}, dimensions={0}, use_global_device_ids=true | all-gather | bytes 73728 | tf_op jit(solution)/shard_map/all_gather | solution.py:20
  232.5 5.4 while.57
  238.8 3.8 fusion.59
  252.2 3.8 fusion.16
  260.5 4.4 copy.146
  267.8 9.8 %multiply_convert_fusion = bf16[1,512,2048]{2,0,1:T(2,128)(2,1)} fusion(f32[1,512,2048]{2,0,1:T(1,128)} %bitcast.151, f32[1,512,2048]{2,0,1:T(1,128)} %bitcast.150), kind=kLoop, calls=%fused_computation.34 | loop fusion | flops 2097152 | bytes 10485760 | tf_op jit(solution)/shard_map/convert_element_type | solution.py:125
  283.4 9.9 %pad_maximum_fusion = bf16[1,512,4096]{2,0,1:T(2,128)(2,1)S(1)} fusion(bf16[1,512,2048]{2,0,1:T(2,128)(2,1)S(1)} %copy-done.2, bf16[1,512,1024]{2,0,1:T(2,128)(2,1)S(1)} %copy.148, bf16[1,512,1024]{2,0,1:T(2,128)(2,1)S(1)} %copy.147), kind=kLoop, calls=%fused_computation.13 | loop fusion | flops 12582912 | bytes 8388608 | tf_op jit(solution)/shard_map/concatenate | solution.py:144
  293.3 3.2 copy-done.5
  296.6 15.4 %convolution_bitcast_fusion = f32[1024,4096]{0,1:T(8,128)} fusion(bf16[1,512,4096]{2,0,1:T(2,128)(2,1)S(1)} %pad_maximum_fusion, bf16[1,512,1024]{2,1,0:T(8,128)(2,1)S(1)} %copy-done), kind=kOutput, calls=%fused_computation.12 | convolution fusion | flops 4294967296 | bytes 22020096 | tf_op jit(solution)/shard_map/dot_general | solution.py:151
  312.1 146.3 %reduce-scatter.2.cloned.1.call-done = f32[256,4096]{0,1:T(8,128)} async-done(((f32[1024,4096]{0,1:T(8,128)}), f32[256,4096]{0,1:T(8,128)}) %reduce-scatter.2.cloned.1.call-update) | async-done | bytes 4194320 | tf_op jit(solution)/shard_map/reduce_scatter | solution.py:154
  461.1 4.4 convert_element_type.52
  465.4 14.2 %fusion.44 = bf16[1,512,1024]{2,1,0:T(8,128)(2,1)} fusion(bf16[1024,4096]{1,0:T(8,128)(2,1)} %all-gather.4.cloned.1.call-done, bf16[1,512,4096]{2,0,1:T(2,128)(2,1)} %copy-done.5), kind=kOutput, calls=%fused_computation.64 | convolution fusion | flops 4295491584 | bytes 13631488 | tf_op jit(solution)/shard_map/dot_general | solution.py:147
  479.7 361.8 %all-reduce.2.cloned.1.call-done = f32[256,4096]{0,1:T(8,128)} async-done(((f32[256,4096]{0,1:T(8,128)}), f32[256,4096]{0,1:T(8,128)}) %all-reduce.2.cloned.1.call-update) | async-done | bytes 4194320 | tf_op jit(solution)/shard_map/psum | solution.py:155
  (155 shorter events, 61.6 us)
Async XLA Ops:
  7.2 85.9 %copy-start = (bf16[1,512,1024]{2,1,0:T(8,128)(2,1)S(1)}, bf16[1,512,1024]{2,1,0:T(8,128)(2,1)}, u32[]{:S(2)}) copy-start(bf16[1,512,1024]{2,1,0:T(8,128)(2,1)} %param.15) | copy-start | bytes 3145732
  7.2 3.4 copy-start.11
  7.2 85.9 %all-gather.4.cloned.1.call-start = ((), (), s32[]{:S(2)}) async-start(), calls=%async_computation.1 | async-start | bytes 10485760 | tf_op jit(solution)/shard_map/all_gather | solution.py:47
  10.5 447.9 %reduce-scatter.2.cloned.1.call-start = ((), (), s32[]{:S(2)}) async-start(), calls=%async_computation.2 | async-start | bytes 20971520 | tf_op jit(solution)/shard_map/reduce_scatter | solution.py:154
  100.0 8.6 copy-start.1
  100.7 7.8 collective-permute-start
  110.1 2.8 copy-start.18
  161.7 22.8 %copy-start.22 = (f32[1,4,16]{2,1,0:T(4,128)}, f32[1,4,16]{2,1,0:T(4,128)S(1)}, u32[]{:S(2)}) copy-start(f32[1,4,16]{2,1,0:T(4,128)S(1)} %reduce_window_sum.28) | copy-start | bytes 772
  187.4 50.5 %copy-start.13 = (f32[4,128,16]{2,1,0:T(8,128)S(1)}, f32[4,128,16]{2,1,0:T(8,128)}, u32[]{:S(2)}) copy-start(f32[4,128,16]{2,1,0:T(8,128)} %get-tuple-element.508) | copy-start | bytes 98308
  245.1 2.2 copy-start.12
  247.4 3.5 copy-start.3
  247.4 4.7 copy-start.8
  252.1 3.9 copy-start.26
  252.1 4.0 copy-start.24
  252.1 4.0 copy-start.15
  252.1 4.0 copy-start.17
  252.1 4.0 copy-start.21
  259.2 22.5 %collective-permute-start.1 = (bf16[1,1,1024]{2,1,0:T(2,128)(2,1)S(1)}, bf16[1,1,1024]{2,1,0:T(2,128)(2,1)S(1)}, u32[]{:S(2)}, u32[]{:S(2)}) collective-permute-start(bf16[1,1,1024]{2,1,0:T(2,128)(2,1)S(1)} %slice.78), channel_id=1, source_target_pairs={{1,0},{2,1},{3,2},{4,3},{5,4},{6,5},{7,6},{9,8},{10,9},{11,10},{12... | collective-permute-start | bytes 6152 | tf_op jit(solution)/shard_map/ppermute | solution.py:13
  260.5 4.4 copy-start.19
  267.8 9.8 %copy-start.20 = (f32[512]{0:T(512)S(1)}, f32[512]{0:T(512)}, u32[]{:S(2)}) copy-start(f32[512]{0:T(512)} %get-tuple-element.511) | copy-start | bytes 6148
  280.0 3.4 copy-start.2
  293.3 3.2 copy-start.5
  312.0 146.4 %copy-start.4 = (bf16[1,4,128,16,128]{4,2,3,1,0:T(8,128)(2,1)S(1)}, bf16[1,4,128,16,128]{4,2,3,1,0:T(8,128)(2,1)}, u32[]{:S(2)}) copy-start(bf16[1,4,128,16,128]{4,2,3,1,0:T(8,128)(2,1)} %get-tuple-element.501) | copy-start | bytes 6291460
  312.0 529.4 %all-reduce.2.cloned.1.call-start = ((), (), s32[]{:S(2)}) async-start(), calls=%async_computation.3 | async-start | bytes 8388608 | tf_op jit(solution)/shard_map/psum | solution.py:155
  (9 other events, 14.0 us)
Sparse Core Ops, SparseCore 0:
  10.6 82.4 all-gather.3
  312.1 146.1 reduce-scatter.1
  460.9 380.5 all-reduce.1
where the time goes:
time: 864 us; the launch traced here: 856 us
  waiting for transfers between devices  588 us (68%)
  blocking collectives  92 us (11%)
  local copies, waits for them, and re-layouts  58.6 us (7%)
  matrix products  49.4 us (6%)
  other arithmetic  46.9 us (5%)
  between operations  14.5 us (2%)
    psum x1, waiting for transfers between devices, per_device(): summed = lax.psum(reduced, ('dp', 'ctx'))  362 us
    reduce_scatter x1, waiting for transfers between devices, per_device(): reduced = lax.psum_scatter(grads, 'fsdp', scatter_dimension=0, tiled=True)  146 us
    all_gather x3, blocking collectives, carried_in(): gathered = jax.tree.map(lambda a: lax.all_gather(a, axis), part)  92 us
    all_gather x1, waiting for transfers between devices, per_device(): full_panels = lax.all_gather(panels, 'fsdp', axis=0, tiled=True)  79.9 us
    unnamed x60, local copies, waits for them, and re-layouts  20.7 us
  transfers between devices with their start and end apart: 5, of which 3 were waited for; matrix products, arithmetic and copies ran while one was open for 6% of the time, Pallas kernels for 0%

commit v1 on v0

--- a/solution.py
+++ b/solution.py
@@ -152,7 +152,7 @@
         flat_tokens, d_all, (((0,), (0,)), ((), ())), preferred_element_type=jnp.float32
     )
     reduced = lax.psum_scatter(grads, "fsdp", scatter_dimension=0, tiled=True)
-    summed = lax.psum(reduced, ("dp", "ctx"))
+    summed = lax.psum(lax.psum(reduced, "dp"), "ctx")
     return (
         dechunked,
         grad_tokens,

time: 864 us -> 765 us (0.89)
  waiting for transfers between devices: 588 us -> 488 us
    psum x1 -> x2, waiting for transfers between devices: 362 us -> 262 us  [per_device(): summed = lax.psum(lax.psum(reduced, 'dp'), 'ctx')]
  transfers between devices with their start and end apart: 5 -> 6, of which waited for: 3 -> 4; matrix products, arithmetic and copies ran while one was open for 6% -> 6% of each run, Pallas kernels for 0% -> 0%
where the time goes in v1:
time: 765 us; the launch traced here: 756 us
  waiting for transfers between devices  488 us (64%)
  blocking collectives  92 us (12%)
  local copies, waits for them, and re-layouts  58.6 us (8%)
  matrix products  49.7 us (6%)
  other arithmetic  46.9 us (6%)
  between operations  14.5 us (2%)
    psum x2, waiting for transfers between devices, per_device(): summed = lax.psum(lax.psum(reduced, 'dp'), 'ctx')  262 us
    reduce_scatter x1, waiting for transfers between devices, per_device(): reduced = lax.psum_scatter(grads, 'fsdp', scatter_dimension=0, tiled=True)  146 us
    all_gather x3, blocking collectives, carried_in(): gathered = jax.tree.map(lambda a: lax.all_gather(a, axis), part)  92 us
    all_gather x1, waiting for transfers between devices, per_device(): full_panels = lax.all_gather(panels, 'fsdp', axis=0, tiled=True)  79.9 us
    unnamed x60, local copies, waits for them, and re-layouts  20.7 us
    dot_general x1, matrix products, per_device(): lax.dot_general(flat_tokens, d_all, (((0,), (0,)), ((), ())), preferred_e...  15.4 us
  transfers between devices with their start and end apart: 6, of which 4 were waited for; matrix products, arithmetic and copies ran while one was open for 6% of the time, Pallas kernels for 0%

profile of v1, /device:TPU:0, one launch (start us, length us, event | category | flops | bytes accessed | tf_op | source)
XLA Modules:
  0.0 756.4 jit_solution(11619156326138579012)
XLA Ops:
  7.2 3.2 pad_maximum_fusion.2
  13.1 79.9 %all-gather.4.cloned.1.call-done = bf16[1024,4096]{1,0:T(8,128)(2,1)} async-done(((bf16[256,4096]{1,0:T(8,128)(2,1)}), bf16[1024,4096]{1,0:T(8,128)(2,1)}) %all-gather.4.cloned.1.call-update) | async-done | bytes 8388624 | tf_op jit(solution)/shard_map/all_gather | solution.py:47
  93.1 6.9 convolution_bitcast_fusion.1
  100.7 4.6 collective-permute-start
  113.6 7.8 %fusion.21 = f32[1,4,128,16,128]{4,2,3,1,0:T(8,128)S(1)} fusion(f32[4,128,16,128]{3,2,1,0:T(8,128)} %bitcast.152, f32[4,16,128]{2,1,0:T(8,128)S(1)} %get-tuple-element.516, f32[4,16,128]{2,1,0:T(8,128)S(1)} %copy.130, pred[128,128]{1,0:T(8,128)(4,1)S(1)} %iota_compare_fusion.1), kind=kOutput, calls=%fused_computation.38 | convolution fusion | flops 1614807040 | bytes 8470528 | tf_op jit(solution)/shard_map/bnhtu,bnuhc->bnthc/dot_general | solution.py:75
  123.4 2.9 while.58
  126.3 34.6 %all-gather = f32[8,16,128]{2,1,0:T(8,128)S(1)} all-gather(f32[1,16,128]{2,1,0:T(8,128)S(1)} %get-tuple-element.266), channel_id=2, replica_groups=mesh['dp'=4,'fsdp'=4,'ctx'=8] {'ctx'}, dimensions={0}, use_global_device_ids=true | all-gather | bytes 73728 | tf_op jit(solution)/shard_map/all_gather | solution.py:20
  162.2 22.3 %all_gather.22 = f32[8,1,16]{2,1,0:T(1,128)} all-gather(f32[1,1,16]{2,1,0:T(1,128)S(1)} %get-tuple-element.521), channel_id=1, replica_groups=mesh['dp'=4,'fsdp'=4,'ctx'=8] {'ctx'}, dimensions={0}, use_global_device_ids=true | all-gather | bytes 576 | tf_op jit(solution)/shard_map/all_gather | solution.py:20
  187.4 5.0 fusion.18
  194.6 2.9 while.59
  197.5 35.0 %all-gather.1 = f32[8,16,128]{2,1,0:T(8,128)S(1)} all-gather(f32[1,16,128]{2,1,0:T(8,128)S(1)} %get-tuple-element.269), channel_id=3, replica_groups=mesh['dp'=4,'fsdp'=4,'ctx'=8] {'ctx'}, dimensions={0}, use_global_device_ids=true | all-gather | bytes 73728 | tf_op jit(solution)/shard_map/all_gather | solution.py:20
  232.5 5.4 while.57
  238.8 3.8 fusion.59
  252.2 3.8 fusion.16
  260.5 4.4 copy.146
  267.8 9.8 %multiply_convert_fusion = bf16[1,512,2048]{2,0,1:T(2,128)(2,1)} fusion(f32[1,512,2048]{2,0,1:T(1,128)} %bitcast.151, f32[1,512,2048]{2,0,1:T(1,128)} %bitcast.150), kind=kLoop, calls=%fused_computation.34 | loop fusion | flops 2097152 | bytes 10485760 | tf_op jit(solution)/shard_map/convert_element_type | solution.py:125
  283.4 9.9 %pad_maximum_fusion = bf16[1,512,4096]{2,0,1:T(2,128)(2,1)S(1)} fusion(bf16[1,512,2048]{2,0,1:T(2,128)(2,1)S(1)} %copy-done.2, bf16[1,512,1024]{2,0,1:T(2,128)(2,1)S(1)} %copy.148, bf16[1,512,1024]{2,0,1:T(2,128)(2,1)S(1)} %copy.147), kind=kLoop, calls=%fused_computation.13 | loop fusion | flops 12582912 | bytes 8388608 | tf_op jit(solution)/shard_map/concatenate | solution.py:144
  293.3 3.2 copy-done.5
  296.6 15.4 %convolution_bitcast_fusion = f32[1024,4096]{0,1:T(8,128)} fusion(bf16[1,512,4096]{2,0,1:T(2,128)(2,1)S(1)} %pad_maximum_fusion, bf16[1,512,1024]{2,1,0:T(8,128)(2,1)S(1)} %copy-done), kind=kOutput, calls=%fused_computation.12 | convolution fusion | flops 4294967296 | bytes 22020096 | tf_op jit(solution)/shard_map/dot_general | solution.py:151
  312.1 146.3 %reduce-scatter.2.cloned.1.call-done = f32[256,4096]{0,1:T(8,128)} async-done(((f32[1024,4096]{0,1:T(8,128)}), f32[256,4096]{0,1:T(8,128)}) %reduce-scatter.2.cloned.1.call-update) | async-done | bytes 4194320 | tf_op jit(solution)/shard_map/reduce_scatter | solution.py:154
  458.4 96.1 %all-reduce.3.cloned.1.call-done = f32[256,4096]{0,1:T(8,128)} async-done(((f32[256,4096]{0,1:T(8,128)}), f32[256,4096]{0,1:T(8,128)}) %all-reduce.3.cloned.1.call-update) | async-done | bytes 4194320 | tf_op jit(solution)/shard_map/psum | solution.py:155
  557.2 4.4 convert_element_type.52
  561.6 14.5 %fusion.44 = bf16[1,512,1024]{2,1,0:T(8,128)(2,1)} fusion(bf16[1024,4096]{1,0:T(8,128)(2,1)} %all-gather.4.cloned.1.call-done, bf16[1,512,4096]{2,0,1:T(2,128)(2,1)} %copy-done.5), kind=kOutput, calls=%fused_computation.64 | convolution fusion | flops 4295491584 | bytes 13631488 | tf_op jit(solution)/shard_map/dot_general | solution.py:147
  576.1 165.8 %all-reduce.5.cloned.1.call-done = f32[256,4096]{0,1:T(8,128)} async-done(((f32[256,4096]{0,1:T(8,128)}), f32[256,4096]{0,1:T(8,128)}) %all-reduce.5.cloned.1.call-update) | async-done | bytes 4194320 | tf_op jit(solution)/shard_map/psum | solution.py:155
  (158 shorter events, 64.5 us)
Async XLA Ops:
  7.2 85.9 %copy-start = (bf16[1,512,1024]{2,1,0:T(8,128)(2,1)S(1)}, bf16[1,512,1024]{2,1,0:T(8,128)(2,1)}, u32[]{:S(2)}) copy-start(bf16[1,512,1024]{2,1,0:T(8,128)(2,1)} %param.15) | copy-start | bytes 3145732
  7.2 3.4 copy-start.11
  7.2 85.9 %all-gather.4.cloned.1.call-start = ((), (), s32[]{:S(2)}) async-start(), calls=%async_computation.1 | async-start | bytes 10485760 | tf_op jit(solution)/shard_map/all_gather | solution.py:47
  10.5 447.9 %reduce-scatter.2.cloned.1.call-start = ((), (), s32[]{:S(2)}) async-start(), calls=%async_computation.2 | async-start | bytes 20971520 | tf_op jit(solution)/shard_map/reduce_scatter | solution.py:154
  100.0 8.6 %copy-start.1 = (f32[512,4096]{1,0:T(8,128)}, f32[512,4096]{1,0:T(8,128)S(1)}, u32[]{:S(2)}) copy-start(f32[512,4096]{1,0:T(8,128)S(1)} %convolution_bitcast_fusion.1) | copy-start | bytes 25165828
  100.7 7.8 %collective-permute-start = (f32[1,1,1024]{2,1,0:T(1,128)S(1)}, f32[1,1,1024]{2,1,0:T(1,128)S(1)}, u32[]{:S(2)}, u32[]{:S(2)}) collective-permute-start(f32[1,1,1024]{2,1,0:T(1,128)S(1)} %slice.70), channel_id=1, source_target_pairs={{0,1},{1,2},{2,3},{3,4},{4,5},{5,6},{6,7},{8,9},{9,10},{10,11},{11... | collective-permute-start | bytes 12296 | tf_op jit(solution)/shard_map/ppermute | solution.py:13
  110.1 2.8 copy-start.18
  161.7 22.8 %copy-start.22 = (f32[1,4,16]{2,1,0:T(4,128)}, f32[1,4,16]{2,1,0:T(4,128)S(1)}, u32[]{:S(2)}) copy-start(f32[1,4,16]{2,1,0:T(4,128)S(1)} %reduce_window_sum.28) | copy-start | bytes 772
  187.4 50.5 %copy-start.13 = (f32[4,128,16]{2,1,0:T(8,128)S(1)}, f32[4,128,16]{2,1,0:T(8,128)}, u32[]{:S(2)}) copy-start(f32[4,128,16]{2,1,0:T(8,128)} %get-tuple-element.508) | copy-start | bytes 98308
  247.4 3.5 copy-start.3
  247.4 4.7 copy-start.8
  252.1 3.9 copy-start.26
  252.1 4.0 copy-start.24
  252.1 4.0 copy-start.15
  252.1 4.0 copy-start.17
  252.1 4.0 copy-start.21
  259.2 22.5 %collective-permute-start.1 = (bf16[1,1,1024]{2,1,0:T(2,128)(2,1)S(1)}, bf16[1,1,1024]{2,1,0:T(2,128)(2,1)S(1)}, u32[]{:S(2)}, u32[]{:S(2)}) collective-permute-start(bf16[1,1,1024]{2,1,0:T(2,128)(2,1)S(1)} %slice.78), channel_id=1, source_target_pairs={{1,0},{2,1},{3,2},{4,3},{5,4},{6,5},{7,6},{9,8},{10,9},{11,10},{12... | collective-permute-start | bytes 6152 | tf_op jit(solution)/shard_map/ppermute | solution.py:13
  260.5 4.4 copy-start.19
  267.8 9.8 %copy-start.20 = (f32[512]{0:T(512)S(1)}, f32[512]{0:T(512)}, u32[]{:S(2)}) copy-start(f32[512]{0:T(512)} %get-tuple-element.511) | copy-start | bytes 6148
  280.0 3.4 copy-start.2
  293.3 3.2 copy-start.5
  312.0 242.5 %all-reduce.3.cloned.1.call-start = ((), (), s32[]{:S(2)}) async-start(), calls=%async_computation.3 | async-start | bytes 8388608 | tf_op jit(solution)/shard_map/psum | solution.py:155
  458.3 96.2 %copy-start.4 = (bf16[1,4,128,16,128]{4,2,3,1,0:T(8,128)(2,1)S(1)}, bf16[1,4,128,16,128]{4,2,3,1,0:T(8,128)(2,1)}, u32[]{:S(2)}) copy-start(bf16[1,4,128,16,128]{4,2,3,1,0:T(8,128)(2,1)} %get-tuple-element.501) | copy-start | bytes 6291460
  458.4 283.6 %all-reduce.5.cloned.1.call-start = ((), (), s32[]{:S(2)}) async-start(), calls=%async_computation.4 | async-start | bytes 8388608 | tf_op jit(solution)/shard_map/psum | solution.py:155
  (10 other events, 16.2 us)
Sparse Core Ops, SparseCore 0:
  10.6 82.4 all-gather.3
  312.1 146.1 reduce-scatter.1
  460.7 93.7 all-reduce.2
  556.9 185.0 all-reduce.4
